TPU v7x, 1024 devices: a whole 4x4x32 slice. The times are simulated.
1024 devices in a mesh: tensor: 32 (over y, z_hi, core), context: 32 (over z_lo, x).
Axes of the slice: x: 4, y: 4, z: 32 (z_hi: 4, z_lo: 8; z = z_hi * 8 + z_lo), core: 2. Of those that a mesh axis runs over, the one named last changes fastest.
Arguments:
- queries: bfloat16 [8192, 4096], P('tensor', 'context'), parts along dimension 0, may hold values from -6 to 6
- keys: bfloat16 [8192, 4096], P('tensor', 'context'), parts along dimension 0, may hold values from -6 to 6
- values: bfloat16 [8192, 4096], P('tensor', 'context'), parts along dimension 0, may hold values from -6 to 6
- filters: float32 [8192, 4096], P(('tensor', 'context')), parts along dimension 0, may hold values from -1 to 1
- skip: float32 [8192], P('tensor'), parts along dimension 0, may hold values from -3 to 3
Outputs:
- output: bfloat16 [8192, 4096], P('tensor', 'context'), parts along dimension 0
There are 32 independent parts, one for each index of `tensor`. A program takes and returns all parts, laid end to end along the dimension named above; each array names one. Nothing has to cross between parts.
All inputs are finite; a program needn't handle non-finite values.
Results may differ from a plain program's by a relative error of at most 0.008.
Values may be sent and summed in bfloat16 or wider, within the bound.
A program may use at most 32 MiB of HBM per device.

v0:
```python
import math

import jax
import jax.numpy as jnp
from jax import lax
from jax.sharding import PartitionSpec as P

RADIX = 128


def tables(row_count, col_count, period):
    row_ids = lax.broadcasted_iota(jnp.int32, (row_count, col_count), 0)
    col_ids = lax.broadcasted_iota(jnp.int32, (row_count, col_count), 1)
    phases = (row_ids * col_ids % period).astype(jnp.float32) * (2.0 * math.pi / period)
    return (jnp.cos(phases), jnp.sin(phases))


def matmul(form, left, right):
    return jnp.einsum(
        form, left, right, precision=lax.Precision.HIGHEST, preferred_element_type=jnp.float32
    )


def forward(signal, radix_size):
    chan_count, seq_len = signal.shape
    full_len = 2 * seq_len
    section_two = full_len // radix_size
    half_radix = radix_size // 2
    blocked = signal.reshape(chan_count, half_radix, section_two)
    cos_first, sin_first = tables(radix_size, half_radix, radix_size)
    turn_cos, turn_sin = tables(radix_size, section_two, full_len)
    cos_second, sin_second = tables(section_two, section_two, section_two)
    real_part = matmul("ab,cbd->cad", cos_first, blocked)
    imag_part = -matmul("ab,cbd->cad", sin_first, blocked)
    real_part, imag_part = (
        real_part * turn_cos + imag_part * turn_sin,
        imag_part * turn_cos - real_part * turn_sin,
    )
    spec_real = matmul("cad,de->cae", real_part, cos_second) + matmul(
        "cad,de->cae", imag_part, sin_second
    )
    spec_imag = matmul("cad,de->cae", imag_part, cos_second) - matmul(
        "cad,de->cae", real_part, sin_second
    )
    return (spec_real, spec_imag)


def inverse(spec_real, spec_imag, radix_size):
    chan_count, _, section_two = spec_real.shape
    full_len = radix_size * section_two
    half_radix = radix_size // 2
    cos_second, sin_second = tables(section_two, section_two, section_two)
    turn_cos, turn_sin = tables(radix_size, section_two, full_len)
    dual_real = matmul("cad,de->cae", spec_real, cos_second) - matmul(
        "cad,de->cae", spec_imag, sin_second
    )
    dual_imag = matmul("cad,de->cae", spec_imag, cos_second) + matmul(
        "cad,de->cae", spec_real, sin_second
    )
    dual_real, dual_imag = (
        dual_real * turn_cos - dual_imag * turn_sin,
        dual_imag * turn_cos + dual_real * turn_sin,
    )
    cos_last, sin_last = tables(half_radix, radix_size, radix_size)
    result = matmul("ab,cbd->cad", cos_last, dual_real) - matmul("ab,cbd->cad", sin_last, dual_imag)
    return result.reshape(chan_count, half_radix * section_two) / full_len


def convolve(signal, filter_rows, radix_size):
    sig_real, sig_imag = forward(signal.astype(jnp.float32), radix_size)
    filt_real, filt_imag = forward(filter_rows, radix_size)
    prod_real = sig_real * filt_real - sig_imag * filt_imag
    prod_imag = sig_real * filt_imag + sig_imag * filt_real
    return inverse(prod_real, prod_imag, radix_size).astype(jnp.bfloat16)


def per_device(queries, keys, values, filters, skip):
    channels, tok_dev = keys.shape
    shards = lax.axis_size("context")
    local_ch = channels // shards
    gated_input = (keys.astype(jnp.float32) * values.astype(jnp.float32)).astype(jnp.bfloat16)
    stacked = gated_input.reshape(shards, local_ch, tok_dev)
    arrived = lax.all_to_all(stacked, "context", split_axis=0, concat_axis=2, tiled=True)
    convolved = convolve(arrived.reshape(local_ch, -1), filters, RADIX)
    returned = lax.all_to_all(
        convolved.reshape(1, local_ch, -1), "context", split_axis=2, concat_axis=0, tiled=True
    )
    conv_tokens = returned.reshape(channels, tok_dev)
    result = queries.astype(jnp.float32) * (
        conv_tokens.astype(jnp.float32) + skip[:, None] * gated_input.astype(jnp.float32)
    )
    return result.astype(jnp.bfloat16)


def solution(mesh):
    placed = (
        P("tensor", "context"),
        P("tensor", "context"),
        P("tensor", "context"),
        P(("tensor", "context"), None),
        P("tensor"),
    )
    return jax.shard_map(
        per_device, mesh=mesh, in_specs=placed, out_specs=P("tensor", "context"), check_vma=False
    )
```

profile of v0, /device:TPU:2, one launch (start us, length us, event | category | flops | bytes accessed | tf_op | source)
XLA Modules:
  0.0 89.6 jit_solution(2054904559755196853)
XLA Ops:
  0.0 1.5 %fusion.68 = bf16[32,8,128]{2,1,0:T(8,128)(2,1)} fusion(bf16[256,128]{1,0:T(8,128)(2,1)} %param.7, bf16[256,128]{1,0:T(8,128)(2,1)} %param.6), kind=kLoop, calls=%fused_computation.97 | loop fusion | flops 131072 | bytes 196608 | tf_op jit(solution)/shard_map/reshape | solution.py:82
  1.5 16.7 %all-to-all-start = ((bf16[32,8,128]{2,1,0:T(8,128)(2,1)}), bf16[32,8,128]{2,1,0:T(8,128)(2,1)S(1)}, u32[]{:S(2)}, u32[]{:S(2)}) async-start(bf16[32,8,128]{2,1,0:T(8,128)(2,1)} %fusion.68), calls=%async_computation | async-start | bytes 131072 | tf_op jit(solution)/shard_map/all_to_all | solution.py:83
  18.3 1.0 %reshape.65 = f32[8,64,64]{2,1,0:T(8,128)S(1)} reshape(f32[8,4096]{1,0:T(8,128)} %param.8) | data formatting | bytes 262144 | tf_op jit(solution)/shard_map/reshape | solution.py:29
  20.5 0.6 fusion.4
  21.1 0.6 fusion.8
  21.6 0.6 convolution_subtract_fusion.2
  22.2 0.6 convolution_add_fusion.1
  22.8 7.2 %all-to-all-done = bf16[32,8,128]{2,1,0:T(8,128)(2,1)S(1)} async-done(((bf16[32,8,128]{2,1,0:T(8,128)(2,1)}), bf16[32,8,128]{2,1,0:T(8,128)(2,1)S(1)}, u32[]{:S(2)}, u32[]{:S(2)}) %all-to-all-start) | async-done | bytes 65568 | tf_op jit(solution)/shard_map/all_to_all | solution.py:83
  30.9 0.5 fusion.24
  31.5 0.5 fusion.23
  32.0 0.6 convolution_add_fusion.2
  32.6 0.6 multiply_subtract_fusion
  33.2 0.5 fusion.45
  33.7 0.5 fusion.43
  34.3 0.5 convolution_subtract_fusion.1
  34.8 0.5 convolution_add_fusion
  36.7 2.8 %copy.20 = bf16[1,8,4096]{1,0,2:T(2,128)(2,1)S(1)} copy(bf16[1,8,4096]{2,1,0:T(8,128)(2,1)S(1)} %convert_element_type.133) | data formatting | bytes 131072 | tf_op jit(solution)/shard_map/convert_element_type | solution.py:74
  40.0 22.6 %reduce = bf16[4096,8]{1,0:T(8,128)(2,1)S(1)} reduce(bf16[4096,1,8]{2,1,0:T(2,128)(2,1)S(1)} %bitcast.90, bf16[]{:T(256)} %broadcast.227), dimensions={1}, to_apply=%bitcast.77.reduce_sub_computation | reduce | bytes 131074
  62.6 1.1 %reshape.78 = bf16[32,2,512]{2,1,0:T(2,128)(2,1)S(1)} reshape(bf16[4096,8]{1,0:T(8,128)(2,1)S(1)} %reduce) | data formatting | bytes 131072
  63.7 17.0 %all_to_all.24 = bf16[32,2,512]{2,1,0:T(2,128)(2,1)S(1)} all-to-all(bf16[32,2,512]{2,1,0:T(2,128)(2,1)S(1)} %reshape.78), channel_id=1, replica_groups=mesh['tensor'=32,'context'=32] {'context'}, dimensions={0} | all-to-all | bytes 131072 | tf_op jit(solution)/shard_map/all_to_all | solution.py:85
  80.7 2.8 %reshape.79 = bf16[4096,1,8]{2,1,0:T(2,128)(2,1)S(1)} reshape(bf16[32,2,512]{2,1,0:T(2,128)(2,1)S(1)} %all_to_all.24) | data formatting | bytes 131072
  83.4 3.2 %bitcast_convert_fusion = f32[1,8,4096]{1,0,2:T(1,128)} fusion(bf16[4096,1,8]{2,1,0:T(2,128)(2,1)S(1)} %reshape.79), kind=kLoop, calls=%fused_computation.178 | loop fusion | flops 32768 | bytes 196608 | tf_op jit(solution)/shard_map/convert_element_type | solution.py:90
  86.7 2.2 %copy.21 = f32[32,1,8,128]{3,2,0,1:T(8,128)S(1)} copy(f32[32,1,8,128]{2,3,0,1:T(8,128)} %bitcast.91) | data formatting | bytes 262144 | tf_op jit(solution)/shard_map/convert_element_type | solution.py:90
  88.9 0.7 fusion.18
  (21 shorter events, 4.0 us)
Async XLA Ops:
  1.5 28.4 %all-to-all-start = ((bf16[32,8,128]{2,1,0:T(8,128)(2,1)}), bf16[32,8,128]{2,1,0:T(8,128)(2,1)S(1)}, u32[]{:S(2)}, u32[]{:S(2)}) async-start(bf16[32,8,128]{2,1,0:T(8,128)(2,1)} %fusion.68), calls=%async_computation | async-start | bytes 131072 | tf_op jit(solution)/shard_map/all_to_all | solution.py:83
  86.7 2.2 %copy-start = (bf16[256,128]{1,0:T(8,128)(2,1)S(1)}, bf16[256,128]{1,0:T(8,128)(2,1)}, u32[]{:S(2)}) copy-start(bf16[256,128]{1,0:T(8,128)(2,1)} %param.7) | copy-start | bytes 196612
  86.7 2.2 %copy-start.1 = (bf16[256,128]{1,0:T(8,128)(2,1)S(1)}, bf16[256,128]{1,0:T(8,128)(2,1)}, u32[]{:S(2)}) copy-start(bf16[256,128]{1,0:T(8,128)(2,1)} %param.6) | copy-start | bytes 196612
  86.7 2.2 %copy-start.2 = (bf16[256,128]{1,0:T(8,128)(2,1)S(1)}, bf16[256,128]{1,0:T(8,128)(2,1)}, u32[]{:S(2)}) copy-start(bf16[256,128]{1,0:T(8,128)(2,1)} %param.5) | copy-start | bytes 196612
  86.7 2.2 %copy-start.3 = (f32[256]{0:T(256)S(1)}, f32[256]{0:T(256)}, u32[]{:S(2)}) copy-start(f32[256]{0:T(256)} %param.9) | copy-start | bytes 3076
where the time goes:
time: 89.9 us; the launch traced here: 89.6 us
  other arithmetic  28.2 us (31%)
  blocking collectives  17 us (19%)
  starting transfers between devices  16.7 us (19%)
  local copies, waits for them, and re-layouts  11 us (12%)
  matrix products  9.43 us (10%)
  waiting for transfers between devices  7.18 us (8%)
    unnamed x1, other arithmetic  22.6 us
    all_to_all x1, blocking collectives, per_device(): lax.all_to_all(convolved.reshape(1, local_ch, -1), 'context', split_axis=...  17 us
    all_to_all x1, starting transfers between devices, per_device(): lax.all_to_all(stacked, 'context', split_axis=0, concat_axis=2, tiled=True)  16.7 us
    dot_general x16, matrix products, matmul(): jnp.einsum(form, left, right, precision=lax.Precision.HIGHEST, preferred_...  8.44 us
    all_to_all x1, waiting for transfers between devices, per_device(): lax.all_to_all(stacked, 'context', split_axis=0, concat_axis=2, tiled=True)  7.18 us
    unnamed x11, local copies, waits for them, and re-layouts  4.43 us
    convert_element_type x1, other arithmetic, per_device(): conv_tokens.astype(jnp.float32)  3.23 us
    convert_element_type x3, local copies, waits for them, and re-layouts, convolve(): return inverse(prod_real, prod_imag, radix_size).astype(jnp.bfloat16)  3.08 us
  transfers between devices with their start and end apart: 1, of which 1 were waited for; matrix products, arithmetic and copies ran while one was open for 5% of the time, Pallas kernels for 0%

commit v1 on v0

v1 whole, which is shorter than its diff:
```python
import functools

import jax
import jax.numpy as jnp
from jax import lax
from jax.experimental import pallas as pl
from jax.experimental.pallas import tpu as pltpu
from jax.sharding import PartitionSpec as P

MESH = pl.DeviceIdType.MESH
EARLY = 3


def conv_kernel(
    keys_hbm,
    values_hbm,
    filters_hbm,
    conv_ref,
    gated_ref,
    keys_ref,
    values_ref,
    taps_ref,
    toep_ref,
    arrived_ref,
    padded_ref,
    mixed_ref,
    outgoing_ref,
    load_sem,
    send_sem,
    recv_sem,
    back_send_sem,
    back_recv_sem,
):
    shards, local_ch, block = gated_ref.shape
    me = lax.axis_index("context")
    tensor = lax.axis_index("tensor")
    barrier = pltpu.get_barrier_semaphore()

    def greet(k, carry):
        peer = lax.rem(me + k, shards)
        pl.semaphore_signal(barrier, inc=1, device_id=(tensor, peer), device_id_type=MESH)
        return carry

    lax.fori_loop(1, shards, greet, 0)

    key_load = pltpu.make_async_copy(keys_hbm, keys_ref, load_sem.at[0])
    value_load = pltpu.make_async_copy(values_hbm, values_ref, load_sem.at[1])
    tap_load = pltpu.make_async_copy(filters_hbm, taps_ref, load_sem.at[2])
    key_load.start()
    value_load.start()
    tap_load.start()
    padded_ref[pl.ds(0, (shards - 1) * local_ch), :] = jnp.zeros(
        ((shards - 1) * local_ch, block), jnp.float32
    )
    key_load.wait()
    value_load.wait()
    gated_ref[...] = (
        keys_ref[...].astype(jnp.float32) * values_ref[...].astype(jnp.float32)
    ).astype(jnp.bfloat16)
    tap_load.wait()

    row_ids = lax.broadcasted_iota(jnp.int32, (block, block), 0)
    col_ids = lax.broadcasted_iota(jnp.int32, (block, block), 1)
    same_block = col_ids >= row_ids

    def build(c):
        def step(d, before):
            start = pl.multiple_of(d * block, block)
            row = taps_ref[c : c + 1, pl.ds(start, block)]
            turned = pltpu.roll(
                jnp.broadcast_to(row, (block, block)), 0, 1, stride=1, stride_axis=0
            )
            toep_ref[c, pl.ds(start, block), :] = jnp.where(same_block, turned, before).astype(
                jnp.bfloat16
            )
            return turned

        lax.fori_loop(0, shards, step, jnp.zeros((block, block), jnp.float32))

    for c in range(EARLY):
        build(c)
    pl.semaphore_wait(barrier, shards - 1)

    def send_out(k, carry):
        peer = lax.rem(me + k, shards)
        pltpu.make_async_remote_copy(
            src_ref=gated_ref.at[peer],
            dst_ref=arrived_ref.at[me],
            send_sem=send_sem,
            recv_sem=recv_sem,
            device_id=(tensor, peer),
            device_id_type=MESH,
        ).start()
        return carry

    lax.fori_loop(1, shards, send_out, 0)
    own = pltpu.make_async_copy(gated_ref.at[me], arrived_ref.at[me], recv_sem)
    own.start()
    for c in range(EARLY, local_ch):
        build(c)
    pltpu.make_async_copy(arrived_ref, arrived_ref, recv_sem).wait()

    padded_ref[pl.ds((shards - 1) * local_ch, shards * local_ch), :] = (
        arrived_ref[...].astype(jnp.float32).reshape(shards * local_ch, block)
    )

    for c in range(local_ch):
        shifted = jnp.concatenate(
            [
                padded_ref[pl.ds((shards - 1 - d) * local_ch + c, shards, stride=local_ch), :]
                for d in range(shards)
            ],
            axis=1,
        ).astype(jnp.bfloat16)
        mixed_ref[pl.ds(c, shards, stride=local_ch), :] = jnp.dot(
            shifted, toep_ref[c], preferred_element_type=jnp.float32
        )
    outgoing_ref[...] = (
        mixed_ref[...].reshape(shards, local_ch, block).astype(jnp.bfloat16)
    )

    def send_back(k, carry):
        peer = lax.rem(me + k, shards)
        pltpu.make_async_remote_copy(
            src_ref=outgoing_ref.at[peer],
            dst_ref=conv_ref.at[me],
            send_sem=back_send_sem,
            recv_sem=back_recv_sem,
            device_id=(tensor, peer),
            device_id_type=MESH,
        ).start()
        return carry

    lax.fori_loop(1, shards, send_back, 0)
    own_back = pltpu.make_async_copy(outgoing_ref.at[me], conv_ref.at[me], back_recv_sem)
    own_back.start()
    others = arrived_ref.at[pl.ds(0, shards - 1)]
    pltpu.make_async_copy(others, others, send_sem).wait()
    pltpu.make_async_copy(conv_ref, conv_ref, back_recv_sem).wait()
    pltpu.make_async_copy(others, others, back_send_sem).wait()


def per_device(queries, keys, values, filters, skip):
    channels, block = keys.shape
    shards = lax.axis_size("context")
    local_ch = channels // shards
    stacked = (shards, local_ch, block)
    vmem = pl.BlockSpec(memory_space=pltpu.VMEM)
    anywhere = pl.BlockSpec(memory_space=pltpu.HBM)
    conv, gated = pl.pallas_call(
        conv_kernel,
        out_shape=(
            jax.ShapeDtypeStruct(stacked, jnp.bfloat16),
            jax.ShapeDtypeStruct(stacked, jnp.bfloat16),
        ),
        in_specs=[anywhere] * 3,
        out_specs=(vmem, vmem),
        scratch_shapes=[
            pltpu.VMEM(stacked, jnp.bfloat16),
            pltpu.VMEM(stacked, jnp.bfloat16),
            pltpu.VMEM((local_ch, shards * block), jnp.float32),
            pltpu.VMEM((local_ch, shards * block, block), jnp.bfloat16),
            pltpu.VMEM(stacked, jnp.bfloat16),
            pltpu.VMEM(((2 * shards - 1) * local_ch, block), jnp.float32),
            pltpu.VMEM((shards * local_ch, block), jnp.float32),
            pltpu.VMEM(stacked, jnp.bfloat16),
            pltpu.SemaphoreType.DMA((3,)),
            pltpu.SemaphoreType.DMA,
            pltpu.SemaphoreType.DMA,
            pltpu.SemaphoreType.DMA,
            pltpu.SemaphoreType.DMA,
        ],
        compiler_params=pltpu.CompilerParams(
            collective_id=0, has_side_effects=True, vmem_limit_bytes=66500000
        ),
        name="hyena_conv",
    )(keys.reshape(stacked), values.reshape(stacked), filters)
    result = queries.astype(jnp.float32) * (
        conv.reshape(channels, block).astype(jnp.float32)
        + skip[:, None] * gated.reshape(channels, block).astype(jnp.float32)
    )
    return result.astype(jnp.bfloat16)


def solution(mesh):
    placed = (
        P("tensor", "context"),
        P("tensor", "context"),
        P("tensor", "context"),
        P(("tensor", "context"), None),
        P("tensor"),
    )
    return jax.shard_map(
        per_device, mesh=mesh, in_specs=placed, out_specs=P("tensor", "context"), check_vma=False
    )
```

time: 89.9 us -> 44.4 us (0.49)
  the two profiles are of different devices: /device:TPU:2 before, /device:TPU:1 now
where the time goes in v1:
time: 44.4 us; the launch traced here: 44.1 us
  Pallas kernels  41.8 us (94%)
  other arithmetic  1.6 us (4%)
  local copies, waits for them, and re-layouts  0.67 us (2%)
    pallas_call x1, Pallas kernels, per_device(): pl.pallas_call(conv_kernel, out_shape=(jax.ShapeDtypeStruct(stacked, jnp....  41.8 us
    convert_element_type x1, other arithmetic, per_device(): return result.astype(jnp.bfloat16)  1.6 us

profile of v1, /device:TPU:1, one launch (start us, length us, event | category | flops | bytes accessed | tf_op | source)
XLA Modules:
  0.0 44.1 jit_solution(8751133238463801270)
XLA Ops:
  0.0 0.0 copy-start
  0.0 41.8 %hyena_conv.1 = (bf16[32,8,128]{2,1,0:T(8,128)(2,1)}, bf16[32,8,128]{2,1,0:T(8,128)(2,1)}) custom-call(bf16[32,8,128]{2,1,0:T(8,128)(2,1)} %bitcast.8, bf16[32,8,128]{2,1,0:T(8,128)(2,1)} %bitcast.9, f32[8,4096]{1,0:T(8,128)} %filters_hbm.1), custom_call_target="tpu_custom_call" | custom-call | tf_op jit(solution)/shard_map/hyena_conv/pallas_call | solution.py:150
  41.8 0.0 copy-start.1
  41.8 0.0 copy-done
  41.9 0.7 %copy-done.1 = f32[256]{0:T(256)S(1)} copy-done((f32[256]{0:T(256)S(1)}, f32[256]{0:T(256)}, u32[]{:S(2)}) %copy-start.1) | copy-done | bytes 1048
  42.5 1.6 %fusion.2 = bf16[256,128]{1,0:T(8,128)(2,1)} fusion(bf16[256,128]{1,0:T(8,128)(2,1)S(1)} %copy-done, bf16[32,8,128]{2,1,0:T(8,128)(2,1)} %get-tuple-element.8, bf16[32,8,128]{2,1,0:T(8,128)(2,1)} %get-tuple-element.7, f32[256]{0:T(256)S(1)} %copy-done.1), kind=kLoop, calls=%fused_computation.3 | loop fusion | flops 229376 | bytes 263168 | tf_op jit(solution)/shard_map/convert_element_type | solution.py:182
Async XLA Ops:
  0.0 41.8 %copy-start = (bf16[256,128]{1,0:T(8,128)(2,1)S(1)}, bf16[256,128]{1,0:T(8,128)(2,1)}, u32[]{:S(2)}) copy-start(bf16[256,128]{1,0:T(8,128)(2,1)} %param.5) | copy-start | bytes 196612
  41.8 0.7 %copy-start.1 = (f32[256]{0:T(256)S(1)}, f32[256]{0:T(256)}, u32[]{:S(2)}) copy-start(f32[256]{0:T(256)} %param.9) | copy-start | bytes 3076

commit v2 on v1

--- a/solution.py
+++ b/solution.py
@@ -8,15 +8,18 @@
 from jax.sharding import PartitionSpec as P
 
 MESH = pl.DeviceIdType.MESH
-EARLY = 3
+EARLY = 4
 
 
 def conv_kernel(
     keys_hbm,
     values_hbm,
     filters_hbm,
+    skip_hbm,
     conv_ref,
+    skipped_ref,
     gated_ref,
+    skip_ref,
     keys_ref,
     values_ref,
     taps_ref,
@@ -34,6 +37,7 @@
     shards, local_ch, block = gated_ref.shape
     me = lax.axis_index("context")
     tensor = lax.axis_index("tensor")
+    upper = me // (shards // 2)
     barrier = pltpu.get_barrier_semaphore()
 
     def greet(k, carry):
@@ -49,6 +53,8 @@
     key_load.start()
     value_load.start()
     tap_load.start()
+    skip_load = pltpu.make_async_copy(skip_hbm, skip_ref, load_sem.at[3])
+    skip_load.start()
     padded_ref[pl.ds(0, (shards - 1) * local_ch), :] = jnp.zeros(
         ((shards - 1) * local_ch, block), jnp.float32
     )
@@ -64,36 +70,37 @@
     same_block = col_ids >= row_ids
 
     def build(c):
-        def step(d, before):
-            start = pl.multiple_of(d * block, block)
-            row = taps_ref[c : c + 1, pl.ds(start, block)]
+        before = jnp.zeros((block, block), jnp.float32)
+        for d in range(shards):
+            row = taps_ref[c : c + 1, d * block : (d + 1) * block]
             turned = pltpu.roll(
                 jnp.broadcast_to(row, (block, block)), 0, 1, stride=1, stride_axis=0
             )
-            toep_ref[c, pl.ds(start, block), :] = jnp.where(same_block, turned, before).astype(
-                jnp.bfloat16
-            )
-            return turned
-
-        lax.fori_loop(0, shards, step, jnp.zeros((block, block), jnp.float32))
+            toep_ref[c, d * block : (d + 1) * block, :] = jnp.where(
+                same_block, turned, before
+            ).astype(jnp.bfloat16)
+            before = turned
 
     for c in range(EARLY):
         build(c)
     pl.semaphore_wait(barrier, shards - 1)
 
     def send_out(k, carry):
-        peer = lax.rem(me + k, shards)
-        pltpu.make_async_remote_copy(
-            src_ref=gated_ref.at[peer],
-            dst_ref=arrived_ref.at[me],
-            send_sem=send_sem,
-            recv_sem=recv_sem,
-            device_id=(tensor, peer),
-            device_id_type=MESH,
-        ).start()
+        peer = upper * k + (1 - upper) * (shards - 1 - k)
+
+        @pl.when(peer != me)
+        def _():
+            pltpu.make_async_remote_copy(
+                src_ref=gated_ref.at[peer],
+                dst_ref=arrived_ref.at[me],
+                send_sem=send_sem,
+                recv_sem=recv_sem,
+                device_id=(tensor, peer),
+                device_id_type=MESH,
+            ).start()
         return carry
 
-    lax.fori_loop(1, shards, send_out, 0)
+    lax.fori_loop(0, shards, send_out, 0)
     own = pltpu.make_async_copy(gated_ref.at[me], arrived_ref.at[me], recv_sem)
     own.start()
     for c in range(EARLY, local_ch):
@@ -120,24 +127,36 @@
     )
 
     def send_back(k, carry):
-        peer = lax.rem(me + k, shards)
-        pltpu.make_async_remote_copy(
-            src_ref=outgoing_ref.at[peer],
-            dst_ref=conv_ref.at[me],
-            send_sem=back_send_sem,
-            recv_sem=back_recv_sem,
-            device_id=(tensor, peer),
-            device_id_type=MESH,
-        ).start()
+        peer = upper * k + (1 - upper) * (shards - 1 - k)
+
+        @pl.when(peer != me)
+        def _():
+            pltpu.make_async_remote_copy(
+                src_ref=outgoing_ref.at[peer],
+                dst_ref=conv_ref.at[me],
+                send_sem=back_send_sem,
+                recv_sem=back_recv_sem,
+                device_id=(tensor, peer),
+                device_id_type=MESH,
+            ).start()
         return carry
 
-    lax.fori_loop(1, shards, send_back, 0)
+    lax.fori_loop(0, shards, send_back, 0)
     own_back = pltpu.make_async_copy(outgoing_ref.at[me], conv_ref.at[me], back_recv_sem)
     own_back.start()
     others = arrived_ref.at[pl.ds(0, shards - 1)]
+    skip_load.wait()
+    columns = jnp.broadcast_to(skip_ref[...][None, :], (block, shards * local_ch)).T
+    skipped_ref[...] = columns * gated_ref[...].astype(jnp.float32).reshape(
+        shards * local_ch, block
+    )
     pltpu.make_async_copy(others, others, send_sem).wait()
     pltpu.make_async_copy(conv_ref, conv_ref, back_recv_sem).wait()
     pltpu.make_async_copy(others, others, back_send_sem).wait()
+
+
+def in_hbm(array):
+    return pltpu.with_memory_space_constraint(array, pltpu.HBM)
 
 
 def per_device(queries, keys, values, filters, skip):
@@ -147,16 +166,18 @@
     stacked = (shards, local_ch, block)
     vmem = pl.BlockSpec(memory_space=pltpu.VMEM)
     anywhere = pl.BlockSpec(memory_space=pltpu.HBM)
-    conv, gated = pl.pallas_call(
+    conv, skipped = pl.pallas_call(
         conv_kernel,
         out_shape=(
             jax.ShapeDtypeStruct(stacked, jnp.bfloat16),
-            jax.ShapeDtypeStruct(stacked, jnp.bfloat16),
+            jax.ShapeDtypeStruct((channels, block), jnp.float32),
         ),
-        in_specs=[anywhere] * 3,
+        in_specs=[anywhere] * 4,
         out_specs=(vmem, vmem),
         scratch_shapes=[
             pltpu.VMEM(stacked, jnp.bfloat16),
+            pltpu.VMEM((channels,), jnp.float32),
+            pltpu.VMEM(stacked, jnp.bfloat16),
             pltpu.VMEM(stacked, jnp.bfloat16),
             pltpu.VMEM((local_ch, shards * block), jnp.float32),
             pltpu.VMEM((local_ch, shards * block, block), jnp.bfloat16),
@@ -164,20 +185,19 @@
             pltpu.VMEM(((2 * shards - 1) * local_ch, block), jnp.float32),
             pltpu.VMEM((shards * local_ch, block), jnp.float32),
             pltpu.VMEM(stacked, jnp.bfloat16),
-            pltpu.SemaphoreType.DMA((3,)),
+            pltpu.SemaphoreType.DMA((4,)),
             pltpu.SemaphoreType.DMA,
             pltpu.SemaphoreType.DMA,
             pltpu.SemaphoreType.DMA,
             pltpu.SemaphoreType.DMA,
         ],
         compiler_params=pltpu.CompilerParams(
-            collective_id=0, has_side_effects=True, vmem_limit_bytes=66500000
+            collective_id=0, has_side_effects=True, vmem_limit_bytes=40 << 20
         ),
         name="hyena_conv",
-    )(keys.reshape(stacked), values.reshape(stacked), filters)
+    )(*(in_hbm(x) for x in (keys.reshape(stacked), values.reshape(stacked), filters, skip)))
     result = queries.astype(jnp.float32) * (
-        conv.reshape(channels, block).astype(jnp.float32)
-        + skip[:, None] * gated.reshape(channels, block).astype(jnp.float32)
+        conv.reshape(channels, block).astype(jnp.float32) + skipped
     )
     return result.astype(jnp.bfloat16)
 

time: 44.4 us -> 32.7 us (0.74)
  the two profiles are of different devices: /device:TPU:1 before, /device:TPU:2 now
where the time goes in v2:
time: 32.7 us; the launch traced here: 32.5 us
  Pallas kernels  31.8 us (97%)
  other arithmetic  0.66 us (2%)
    pallas_call x1, Pallas kernels, per_device(): pl.pallas_call(conv_kernel, out_shape=(jax.ShapeDtypeStruct(stacked, jnp....  31.8 us
    convert_element_type x1, other arithmetic, per_device(): return result.astype(jnp.bfloat16)  0.66 us

profile of v2, /device:TPU:2, one launch (start us, length us, event | category | flops | bytes accessed | tf_op | source)
XLA Modules:
  0.0 32.5 jit_solution(16517699744514417308)
XLA Ops:
  0.0 0.0 copy-start
  0.0 31.8 %hyena_conv.1 = (bf16[32,8,128]{2,1,0:T(8,128)(2,1)S(1)}, f32[256,128]{1,0:T(8,128)S(1)}) custom-call(bf16[32,8,128]{2,1,0:T(8,128)(2,1)} %bitcast.5, bf16[32,8,128]{2,1,0:T(8,128)(2,1)} %bitcast.6, f32[8,4096]{1,0:T(8,128)} %filters_hbm.1, f32[256]{0:T(256)} %skip_hbm.1), custom_call_target="tpu_custom_call" | custom-call | tf_op jit(solution)/shard_map/hyena_conv/pallas_call | solution.py:169
  31.8 0.0 copy-done
  31.8 0.7 %fusion.1 = bf16[256,128]{1,0:T(8,128)(2,1)} fusion(f32[256,128]{1,0:T(8,128)S(1)} %get-tuple-element.8, bf16[256,128]{1,0:T(8,128)(2,1)S(1)} %copy-done, bf16[32,8,128]{2,1,0:T(8,128)(2,1)S(1)} %get-tuple-element.7), kind=kLoop, calls=%fused_computation.2 | loop fusion | flops 163840 | bytes 327680 | tf_op jit(solution)/shard_map/convert_element_type | solution.py:202
Async XLA Ops:
  0.0 31.8 %copy-start = (bf16[256,128]{1,0:T(8,128)(2,1)S(1)}, bf16[256,128]{1,0:T(8,128)(2,1)}, u32[]{:S(2)}) copy-start(bf16[256,128]{1,0:T(8,128)(2,1)} %param.5) | copy-start | bytes 196612

commit v3 on v2

--- a/solution.py
+++ b/solution.py
@@ -8,7 +8,9 @@
 from jax.sharding import PartitionSpec as P
 
 MESH = pl.DeviceIdType.MESH
-EARLY = 4
+EARLY = 2
+FIRST = 8
+SECOND = 16
 
 
 def conv_kernel(
@@ -84,6 +86,7 @@
     for c in range(EARLY):
         build(c)
     pl.semaphore_wait(barrier, shards - 1)
+    mine = recv_sem.at[lax.min(me // FIRST, 2)]
 
     def send_out(k, carry):
         peer = upper * k + (1 - upper) * (shards - 1 - k)
@@ -94,41 +97,19 @@
                 src_ref=gated_ref.at[peer],
                 dst_ref=arrived_ref.at[me],
                 send_sem=send_sem,
-                recv_sem=recv_sem,
+                recv_sem=mine,
                 device_id=(tensor, peer),
                 device_id_type=MESH,
             ).start()
+
         return carry
 
     lax.fori_loop(0, shards, send_out, 0)
-    own = pltpu.make_async_copy(gated_ref.at[me], arrived_ref.at[me], recv_sem)
-    own.start()
+    pltpu.make_async_copy(gated_ref.at[me], arrived_ref.at[me], mine).start()
     for c in range(EARLY, local_ch):
         build(c)
-    pltpu.make_async_copy(arrived_ref, arrived_ref, recv_sem).wait()
-
-    padded_ref[pl.ds((shards - 1) * local_ch, shards * local_ch), :] = (
-        arrived_ref[...].astype(jnp.float32).reshape(shards * local_ch, block)
-    )
-
-    for c in range(local_ch):
-        shifted = jnp.concatenate(
-            [
-                padded_ref[pl.ds((shards - 1 - d) * local_ch + c, shards, stride=local_ch), :]
-                for d in range(shards)
-            ],
-            axis=1,
-        ).astype(jnp.bfloat16)
-        mixed_ref[pl.ds(c, shards, stride=local_ch), :] = jnp.dot(
-            shifted, toep_ref[c], preferred_element_type=jnp.float32
-        )
-    outgoing_ref[...] = (
-        mixed_ref[...].reshape(shards, local_ch, block).astype(jnp.bfloat16)
-    )
-
-    def send_back(k, carry):
-        peer = upper * k + (1 - upper) * (shards - 1 - k)
-
+
+    def send_back(peer):
         @pl.when(peer != me)
         def _():
             pltpu.make_async_remote_copy(
@@ -139,11 +120,39 @@
                 device_id=(tensor, peer),
                 device_id_type=MESH,
             ).start()
-        return carry
-
-    lax.fori_loop(0, shards, send_back, 0)
-    own_back = pltpu.make_async_copy(outgoing_ref.at[me], conv_ref.at[me], back_recv_sem)
-    own_back.start()
+
+    for group, (low, high) in enumerate(((0, FIRST), (FIRST, SECOND), (SECOND, shards))):
+        part = arrived_ref.at[low:high]
+        pltpu.make_async_copy(part, part, recv_sem.at[group]).wait()
+        padded_ref[(shards - 1 + low) * local_ch : (shards - 1 + high) * local_ch, :] = (
+            part[...].astype(jnp.float32).reshape((high - low) * local_ch, block)
+        )
+        for c in range(local_ch):
+            shifted = jnp.concatenate(
+                [
+                    padded_ref[
+                        pl.ds((shards - 1 + low - d) * local_ch + c, high - low, stride=local_ch), :
+                    ]
+                    for d in range(high)
+                ],
+                axis=1,
+            ).astype(jnp.bfloat16)
+            mixed_ref[pl.ds(low * local_ch + c, high - low, stride=local_ch), :] = jnp.dot(
+                shifted, toep_ref[c, : high * block, :], preferred_element_type=jnp.float32
+            )
+        outgoing_ref[low:high] = (
+            mixed_ref[low * local_ch : high * local_ch, :]
+            .reshape(high - low, local_ch, block)
+            .astype(jnp.bfloat16)
+        )
+
+        def send_part(k, carry, low=low, high=high):
+            send_back(upper * (low + k) + (1 - upper) * (high - 1 - k))
+            return carry
+
+        lax.fori_loop(0, high - low, send_part, 0)
+
+    pltpu.make_async_copy(outgoing_ref.at[me], conv_ref.at[me], back_recv_sem).start()
     others = arrived_ref.at[pl.ds(0, shards - 1)]
     skip_load.wait()
     columns = jnp.broadcast_to(skip_ref[...][None, :], (block, shards * local_ch)).T
@@ -187,7 +196,7 @@
             pltpu.VMEM(stacked, jnp.bfloat16),
             pltpu.SemaphoreType.DMA((4,)),
             pltpu.SemaphoreType.DMA,
-            pltpu.SemaphoreType.DMA,
+            pltpu.SemaphoreType.DMA((3,)),
             pltpu.SemaphoreType.DMA,
             pltpu.SemaphoreType.DMA,
         ],

time: 32.7 us -> 30.4 us (0.930)
  Pallas kernels: 31.8 us -> 29.5 us
    pallas_call x1, Pallas kernels: 31.8 us -> 29.5 us  [per_device(): pl.pallas_call(conv_kernel, out_shape=(jax.ShapeDtypeStruct(stacked, jnp....]
where the time goes in v3:
time: 30.4 us; the launch traced here: 30.2 us
  Pallas kernels  29.5 us (97%)
  other arithmetic  0.66 us (2%)
    pallas_call x1, Pallas kernels, per_device(): pl.pallas_call(conv_kernel, out_shape=(jax.ShapeDtypeStruct(stacked, jnp....  29.5 us
    convert_element_type x1, other arithmetic, per_device(): return result.astype(jnp.bfloat16)  0.66 us

profile of v3, /device:TPU:2, one launch (start us, length us, event | category | flops | bytes accessed | tf_op | source)
XLA Modules:
  0.0 30.2 jit_solution(8174009844771159183)
XLA Ops:
  0.0 0.0 copy-start
  0.0 29.5 %hyena_conv.1 = (bf16[32,8,128]{2,1,0:T(8,128)(2,1)S(1)}, f32[256,128]{1,0:T(8,128)S(1)}) custom-call(bf16[32,8,128]{2,1,0:T(8,128)(2,1)} %bitcast.5, bf16[32,8,128]{2,1,0:T(8,128)(2,1)} %bitcast.6, f32[8,4096]{1,0:T(8,128)} %filters_hbm.1, f32[256]{0:T(256)} %skip_hbm.1), custom_call_target="tpu_custom_call" | custom-call | tf_op jit(solution)/shard_map/hyena_conv/pallas_call | solution.py:178
  29.5 0.0 copy-done
  29.6 0.7 %fusion.1 = bf16[256,128]{1,0:T(8,128)(2,1)} fusion(f32[256,128]{1,0:T(8,128)S(1)} %get-tuple-element.8, bf16[256,128]{1,0:T(8,128)(2,1)S(1)} %copy-done, bf16[32,8,128]{2,1,0:T(8,128)(2,1)S(1)} %get-tuple-element.7), kind=kLoop, calls=%fused_computation.2 | loop fusion | flops 163840 | bytes 327680 | tf_op jit(solution)/shard_map/convert_element_type | solution.py:211
Async XLA Ops:
  0.0 29.5 %copy-start = (bf16[256,128]{1,0:T(8,128)(2,1)S(1)}, bf16[256,128]{1,0:T(8,128)(2,1)}, u32[]{:S(2)}) copy-start(bf16[256,128]{1,0:T(8,128)(2,1)} %param.5) | copy-start | bytes 196612

commit v4 on v3

v4 whole, which is shorter than its diff:
```python
import functools

import jax
import jax.numpy as jnp
from jax import lax
from jax.experimental import pallas as pl
from jax.experimental.pallas import tpu as pltpu
from jax.sharding import PartitionSpec as P

MESH = pl.DeviceIdType.MESH
FIRST = 8


def conv_kernel(
    keys_hbm,
    values_hbm,
    filters_hbm,
    skip_hbm,
    conv_ref,
    skipped_ref,
    gated_ref,
    skip_ref,
    keys_ref,
    values_ref,
    taps_ref,
    toep_ref,
    arrived_ref,
    padded_ref,
    mixed_ref,
    outgoing_ref,
    lent_ref,
    borrowed_ref,
    low_toep_ref,
    low_arrived_ref,
    low_padded_ref,
    low_mixed_ref,
    low_outgoing_ref,
    load_sem,
    send_sem,
    recv_sem,
    low_send_sem,
    low_recv_sem,
    lend_sem,
    borrow_sem,
    back_send_sem,
    low_back_send_sem,
    back_recv_sem,
    last_sem,
):
    shards, local_ch, block = gated_ref.shape
    me = lax.axis_index("context")
    tensor = lax.axis_index("tensor")
    half = shards // 2
    upper = me // half
    partner = lax.rem(me + half, shards)
    barrier = pltpu.get_barrier_semaphore()

    first_group = 1 - lax.min(tensor, 1)
    is_last = me + tensor == 0
    alone = (tensor == 0) & (partner == 0)
    borrows = (upper == 0) & (me + tensor > 0)
    lends = (upper == 1) & (partner + tensor > 0)

    def greet(k, carry):
        peer = lax.rem(me + k, shards)
        pl.semaphore_signal(barrier, inc=1, device_id=(tensor, peer), device_id_type=MESH)
        return carry

    @pl.when(jnp.logical_not(is_last))
    def _():
        lax.fori_loop(1, shards, greet, 0)

    key_load = pltpu.make_async_copy(keys_hbm, keys_ref, load_sem.at[0])
    value_load = pltpu.make_async_copy(values_hbm, values_ref, load_sem.at[1])
    tap_load = pltpu.make_async_copy(filters_hbm, taps_ref, load_sem.at[2])
    key_load.start()
    value_load.start()
    tap_load.start()
    skip_load = pltpu.make_async_copy(skip_hbm, skip_ref, load_sem.at[3])
    skip_load.start()
    padded_ref[pl.ds(0, (shards - 1) * local_ch), :] = jnp.zeros(
        ((shards - 1) * local_ch, block), jnp.float32
    )
    low_padded_ref[pl.ds(0, (half - 1) * local_ch), :] = jnp.zeros(
        ((half - 1) * local_ch, block), jnp.float32
    )
    key_load.wait()
    value_load.wait()
    gated_ref[...] = (
        keys_ref[...].astype(jnp.float32) * values_ref[...].astype(jnp.float32)
    ).astype(jnp.bfloat16)
    tap_load.wait()
    for d in range(half):
        lent_ref[d] = taps_ref[:, d * block : (d + 1) * block].astype(jnp.bfloat16)

    row_ids = lax.broadcasted_iota(jnp.int32, (block, block), 0)
    col_ids = lax.broadcasted_iota(jnp.int32, (block, block), 1)
    same_block = col_ids >= row_ids

    def turn(row):
        return pltpu.roll(jnp.broadcast_to(row, (block, block)), 0, 1, stride=1, stride_axis=0)

    def build(row_of, into, c, first, last):
        before = turn(row_of(first - 1)) if first else jnp.zeros((block, block), jnp.float32)
        for d in range(first, last):
            turned = turn(row_of(d))
            into[c, d * block : (d + 1) * block, :] = jnp.where(
                same_block, turned, before
            ).astype(jnp.bfloat16)
            before = turned

    def build_own(c):
        def row_of(d):
            return taps_ref[c : c + 1, d * block : (d + 1) * block]

        build(row_of, toep_ref, c, 0, shards)

    def build_borrowed(first, last):
        for c in range(local_ch):

            def row_of(d, c=c):
                return borrowed_ref[d].astype(jnp.float32)[c : c + 1, :]

            build(row_of, low_toep_ref, c, first, last)

    @pl.when(borrows)
    def _():
        for c in range(local_ch):
            build_own(c)

    pl.semaphore_wait(barrier, shards - 1 - first_group * lax.min(me, 1))

    @pl.when(is_last)
    def _():
        def announce(peer, carry):
            pl.semaphore_signal(last_sem, inc=1, device_id=(tensor, peer), device_id_type=MESH)
            return carry

        lax.fori_loop(1, shards, announce, 0)


    def push(source, target, sent, received, peer):
        pltpu.make_async_remote_copy(
            src_ref=source,
            dst_ref=target,
            send_sem=sent,
            recv_sem=received,
            device_id=(tensor, peer),
            device_id_type=MESH,
        ).start()

    mine = recv_sem.at[me // FIRST]
    low_mine = low_recv_sem.at[lax.rem(me, half) // FIRST]

    def send_out(peer):
        push(gated_ref.at[peer], arrived_ref.at[me], send_sem, mine, peer)

    def send_both(peer):
        push(gated_ref.at[peer + half], low_arrived_ref.at[me], low_send_sem, low_mine, peer)
        send_out(peer)

    def lend():
        push(lent_ref, borrowed_ref, lend_sem, borrow_sem, partner)

    @pl.when(upper == 0)
    def _():
        def send_low(peer, carry):
            @pl.when((peer != me) & (peer + 1 - first_group > 0))
            def _():
                send_both(peer)

            return carry

        def send_high(k, carry):
            send_out(shards - 1 - k)
            return carry

        lax.fori_loop(0, half, send_low, 0)

        @pl.when(borrows)
        def _():
            pltpu.make_async_copy(gated_ref.at[partner], low_arrived_ref.at[me], low_mine).start()

        lax.fori_loop(0, half, send_high, 0)

    @pl.when(upper == 1)
    def _():
        @pl.when(lends)
        def _():
            lend()

        def send_any(peer, carry):
            @pl.when((peer != me) & (peer + 1 - first_group > 0))
            def _():
                send_out(peer)

            return carry

        lax.fori_loop(0, shards, send_any, 0)

    pltpu.make_async_copy(gated_ref.at[me], arrived_ref.at[me], mine).start()

    @pl.when(jnp.logical_not(borrows))
    def _():
        for c in range(local_ch):
            build_own(c)

    @pl.when((tensor == 0) & (me > 0))
    def _():
        pl.semaphore_wait(last_sem, 1)
        send_out(0)

    @pl.when(borrows)
    def _():
        pltpu.make_async_copy(borrowed_ref, borrowed_ref, borrow_sem).wait()
        build_borrowed(0, half)

    def take(arrived, padded, zeros, sem, low, high):
        part = arrived.at[low:high]
        pltpu.make_async_copy(part, part, sem).wait()
        padded[(zeros + low) * local_ch : (zeros + high) * local_ch, :] = (
            part[...].astype(jnp.float32).reshape((high - low) * local_ch, block)
        )

    def convolve(padded, zeros, toep, mixed, outgoing, low, high):
        for c in range(local_ch):
            shifted = jnp.concatenate(
                [
                    padded[pl.ds((zeros + low - d) * local_ch + c, high - low, stride=local_ch), :]
                    for d in range(high)
                ],
                axis=1,
            ).astype(jnp.bfloat16)
            mixed[pl.ds(low * local_ch + c, high - low, stride=local_ch), :] = jnp.dot(
                shifted, toep[c, : high * block, :], preferred_element_type=jnp.float32
            )
        outgoing[low:high] = (
            mixed[low * local_ch : high * local_ch, :]
            .reshape(high - low, local_ch, block)
            .astype(jnp.bfloat16)
        )

    def send_back(outgoing, slot, sent, low, high):
        def one(k, carry):
            peer = upper * (low + k) + (1 - upper) * (high - 1 - k)

            @pl.when(peer != me)
            def _():
                push(outgoing.at[peer], conv_ref.at[slot], sent, back_recv_sem, peer)

            return carry

        lax.fori_loop(0, high - low, one, 0)

    for group, (low, high) in enumerate(((0, FIRST), (FIRST, half))):
        take(arrived_ref, padded_ref, shards - 1, recv_sem.at[group], low, high)

        @pl.when((upper == 0) | alone)
        def _(low=low, high=high):
            convolve(padded_ref, shards - 1, toep_ref, mixed_ref, outgoing_ref, low, high)
            send_back(outgoing_ref, me, back_send_sem, low, high)

        @pl.when(borrows)
        def _(group=group, low=low, high=high):
            take(
                low_arrived_ref, low_padded_ref, half - 1, low_recv_sem.at[group], low, high
            )
            convolve(
                low_padded_ref, half - 1, low_toep_ref, low_mixed_ref, low_outgoing_ref, low, high
            )
            send_back(low_outgoing_ref, partner, low_back_send_sem, low, high)

    for low in range(half, shards, FIRST):
        high = low + FIRST
        take(arrived_ref, padded_ref, shards - 1, recv_sem.at[low // FIRST], low, high)
        convolve(padded_ref, shards - 1, toep_ref, mixed_ref, outgoing_ref, low, high)
        send_back(outgoing_ref, me, back_send_sem, low, high)

    pltpu.make_async_copy(outgoing_ref.at[me], conv_ref.at[me], back_recv_sem).start()

    @pl.when(borrows)
    def _():
        pltpu.make_async_copy(
            low_outgoing_ref.at[me], conv_ref.at[partner], back_recv_sem
        ).start()

    others = arrived_ref.at[pl.ds(0, shards - 1)]
    skip_load.wait()
    columns = jnp.broadcast_to(skip_ref[...][None, :], (block, shards * local_ch)).T
    skipped_ref[...] = columns * gated_ref[...].astype(jnp.float32).reshape(
        shards * local_ch, block
    )
    few = arrived_ref.at[pl.ds(0, half - 1)]
    pltpu.make_async_copy(others, others, send_sem).wait()
    pltpu.make_async_copy(conv_ref, conv_ref, back_recv_sem).wait()

    @pl.when((upper == 0) & ((tensor > 0) | (me == 0)))
    def _():
        pltpu.make_async_copy(few, few, low_send_sem).wait()

    @pl.when((upper == 0) & (tensor == 0) & (me > 0))
    def _():
        fewer = arrived_ref.at[pl.ds(0, half - 2)]
        pltpu.make_async_copy(fewer, fewer, low_send_sem).wait()

    @pl.when(borrows)
    def _():
        pltpu.make_async_copy(few, few, low_back_send_sem).wait()

    @pl.when((upper == 0) | alone)
    def _():
        pltpu.make_async_copy(others, others, back_send_sem).wait()

    @pl.when(lends)
    def _():
        pltpu.make_async_copy(lent_ref, lent_ref, lend_sem).wait()
        pltpu.make_async_copy(few, few, back_send_sem).wait()


def in_hbm(array):
    return pltpu.with_memory_space_constraint(array, pltpu.HBM)


def per_device(queries, keys, values, filters, skip):
    channels, block = keys.shape
    shards = lax.axis_size("context")
    local_ch = channels // shards
    half = shards // 2
    stacked = (shards, local_ch, block)
    vmem = pl.BlockSpec(memory_space=pltpu.VMEM)
    anywhere = pl.BlockSpec(memory_space=pltpu.HBM)
    conv, skipped = pl.pallas_call(
        conv_kernel,
        out_shape=(
            jax.ShapeDtypeStruct(stacked, jnp.bfloat16),
            jax.ShapeDtypeStruct((channels, block), jnp.float32),
        ),
        in_specs=[anywhere] * 4,
        out_specs=(vmem, vmem),
        scratch_shapes=[
            pltpu.VMEM(stacked, jnp.bfloat16),
            pltpu.VMEM((channels,), jnp.float32),
            pltpu.VMEM(stacked, jnp.bfloat16),
            pltpu.VMEM(stacked, jnp.bfloat16),
            pltpu.VMEM((local_ch, shards * block), jnp.float32),
            pltpu.VMEM((local_ch, shards * block, block), jnp.bfloat16),
            pltpu.VMEM(stacked, jnp.bfloat16),
            pltpu.VMEM(((2 * shards - 1) * local_ch, block), jnp.float32),
            pltpu.VMEM((shards * local_ch, block), jnp.float32),
            pltpu.VMEM(stacked, jnp.bfloat16),
            pltpu.VMEM((half, local_ch, block), jnp.bfloat16),
            pltpu.VMEM((half, local_ch, block), jnp.bfloat16),
            pltpu.VMEM((local_ch, half * block, block), jnp.bfloat16),
            pltpu.VMEM((half, local_ch, block), jnp.bfloat16),
            pltpu.VMEM(((2 * half - 1) * local_ch, block), jnp.float32),
            pltpu.VMEM((half * local_ch, block), jnp.float32),
            pltpu.VMEM((half, local_ch, block), jnp.bfloat16),
            pltpu.SemaphoreType.DMA((4,)),
            pltpu.SemaphoreType.DMA,
            pltpu.SemaphoreType.DMA((4,)),
            pltpu.SemaphoreType.DMA,
            pltpu.SemaphoreType.DMA((2,)),
            pltpu.SemaphoreType.DMA,
            pltpu.SemaphoreType.DMA,
            pltpu.SemaphoreType.DMA,
            pltpu.SemaphoreType.DMA,
            pltpu.SemaphoreType.DMA,
            pltpu.SemaphoreType.REGULAR,
        ],
        compiler_params=pltpu.CompilerParams(
            collective_id=0, has_side_effects=True, vmem_limit_bytes=40 << 20
        ),
        name="hyena_conv",
    )(*(in_hbm(x) for x in (keys.reshape(stacked), values.reshape(stacked), filters, skip)))
    result = queries.astype(jnp.float32) * (
        conv.reshape(channels, block).astype(jnp.float32) + skipped
    )
    return result.astype(jnp.bfloat16)


def solution(mesh):
    placed = (
        P("tensor", "context"),
        P("tensor", "context"),
        P("tensor", "context"),
        P(("tensor", "context"), None),
        P("tensor"),
    )
    return jax.shard_map(
        per_device, mesh=mesh, in_specs=placed, out_specs=P("tensor", "context"), check_vma=False
    )
```

time: 30.4 us -> 29.3 us (0.964)
  the two profiles are of different devices: /device:TPU:2 before, /device:TPU:24 now
where the time goes in v4:
time: 29.3 us; the launch traced here: 29.1 us
  Pallas kernels  28.4 us (97%)
  other arithmetic  0.66 us (2%)
    pallas_call x1, Pallas kernels, per_device(): pl.pallas_call(conv_kernel, out_shape=(jax.ShapeDtypeStruct(stacked, jnp....  28.4 us
    convert_element_type x1, other arithmetic, per_device(): return result.astype(jnp.bfloat16)  0.66 us

profile of v4, /device:TPU:24, one launch (start us, length us, event | category | flops | bytes accessed | tf_op | source)
XLA Modules:
  0.0 29.1 jit_solution(10354682681044663743)
XLA Ops:
  0.0 0.0 copy-start
  0.0 28.4 %hyena_conv.1 = (bf16[32,8,128]{2,1,0:T(8,128)(2,1)S(1)}, f32[256,128]{1,0:T(8,128)S(1)}) custom-call(bf16[32,8,128]{2,1,0:T(8,128)(2,1)} %bitcast.5, bf16[32,8,128]{2,1,0:T(8,128)(2,1)} %bitcast.6, f32[8,4096]{1,0:T(8,128)} %filters_hbm.1, f32[256]{0:T(256)} %skip_hbm.1), custom_call_target="tpu_custom_call" | custom-call | tf_op jit(solution)/shard_map/hyena_conv/pallas_call | solution.py:332
  28.5 0.0 copy-done
  28.5 0.7 %fusion.1 = bf16[256,128]{1,0:T(8,128)(2,1)} fusion(f32[256,128]{1,0:T(8,128)S(1)} %get-tuple-element.8, bf16[256,128]{1,0:T(8,128)(2,1)S(1)} %copy-done, bf16[32,8,128]{2,1,0:T(8,128)(2,1)S(1)} %get-tuple-element.7), kind=kLoop, calls=%fused_computation.2 | loop fusion | flops 163840 | bytes 327680 | tf_op jit(solution)/shard_map/convert_element_type | solution.py:378
Async XLA Ops:
  0.0 28.5 %copy-start = (bf16[256,128]{1,0:T(8,128)(2,1)S(1)}, bf16[256,128]{1,0:T(8,128)(2,1)}, u32[]{:S(2)}) copy-start(bf16[256,128]{1,0:T(8,128)(2,1)} %param.5) | copy-start | bytes 196612

commit v5 on v4

--- a/solution.py
+++ b/solution.py
@@ -9,6 +9,7 @@
 
 MESH = pl.DeviceIdType.MESH
 FIRST = 8
+TAIL = 4
 
 
 def conv_kernel(
@@ -149,7 +150,7 @@
             device_id_type=MESH,
         ).start()
 
-    mine = recv_sem.at[me // FIRST]
+    mine = recv_sem.at[me // TAIL]
     low_mine = low_recv_sem.at[lax.rem(me, half) // FIRST]
 
     def send_out(peer):
@@ -252,29 +253,81 @@
 
         lax.fori_loop(0, high - low, one, 0)
 
-    for group, (low, high) in enumerate(((0, FIRST), (FIRST, half))):
-        take(arrived_ref, padded_ref, shards - 1, recv_sem.at[group], low, high)
-
-        @pl.when((upper == 0) | alone)
-        def _(low=low, high=high):
-            convolve(padded_ref, shards - 1, toep_ref, mixed_ref, outgoing_ref, low, high)
-            send_back(outgoing_ref, me, back_send_sem, low, high)
-
-        @pl.when(borrows)
-        def _(group=group, low=low, high=high):
+    def take_own(low, high):
+        for start in range(low, high, TAIL):
             take(
-                low_arrived_ref, low_padded_ref, half - 1, low_recv_sem.at[group], low, high
+                arrived_ref,
+                padded_ref,
+                shards - 1,
+                recv_sem.at[start // TAIL],
+                start,
+                start + TAIL,
             )
-            convolve(
-                low_padded_ref, half - 1, low_toep_ref, low_mixed_ref, low_outgoing_ref, low, high
+
+    take_own(0, half)
+
+    @pl.when((upper == 0) | alone)
+    def _():
+        convolve(padded_ref, shards - 1, toep_ref, mixed_ref, outgoing_ref, 0, half)
+        send_back(outgoing_ref, me, back_send_sem, 0, half)
+
+    @pl.when(borrows)
+    def _():
+        for group in range(half // FIRST):
+            take(
+                low_arrived_ref,
+                low_padded_ref,
+                half - 1,
+                low_recv_sem.at[group],
+                group * FIRST,
+                group * FIRST + FIRST,
             )
-            send_back(low_outgoing_ref, partner, low_back_send_sem, low, high)
-
-    for low in range(half, shards, FIRST):
-        high = low + FIRST
-        take(arrived_ref, padded_ref, shards - 1, recv_sem.at[low // FIRST], low, high)
+        convolve(low_padded_ref, half - 1, low_toep_ref, low_mixed_ref, low_outgoing_ref, 0, half)
+        send_back(low_outgoing_ref, partner, low_back_send_sem, 0, half)
+
+    def upper_rows(low, high):
+        take_own(low, high)
         convolve(padded_ref, shards - 1, toep_ref, mixed_ref, outgoing_ref, low, high)
         send_back(outgoing_ref, me, back_send_sem, low, high)
+
+    @pl.when(is_last)
+    def _():
+        edge = shards - TAIL
+        for low in range(half, shards - FIRST, FIRST):
+            upper_rows(low, low + FIRST)
+        take_own(shards - FIRST, edge)
+        padded_ref[(shards - 1 + edge) * local_ch :, :] = jnp.zeros(
+            (TAIL * local_ch, block), jnp.float32
+        )
+        convolve(
+            padded_ref, shards - 1, toep_ref, mixed_ref, outgoing_ref, shards - FIRST, shards
+        )
+        send_back(outgoing_ref, me, back_send_sem, shards - FIRST, edge)
+        part = arrived_ref.at[edge:shards]
+        pltpu.make_async_copy(part, part, recv_sem.at[edge // TAIL]).wait()
+        low_padded_ref[(half - 1) * local_ch : (half - 1 + TAIL) * local_ch, :] = (
+            part[...].astype(jnp.float32).reshape(TAIL * local_ch, block)
+        )
+        for c in range(local_ch):
+            shifted = jnp.concatenate(
+                [
+                    low_padded_ref[pl.ds((half - 1 - d) * local_ch + c, TAIL, stride=local_ch), :]
+                    for d in range(TAIL)
+                ],
+                axis=1,
+            ).astype(jnp.bfloat16)
+            rows = pl.ds(edge * local_ch + c, TAIL, stride=local_ch)
+            mixed_ref[rows, :] = mixed_ref[rows, :] + jnp.dot(
+                shifted, toep_ref[c, : TAIL * block, :], preferred_element_type=jnp.float32
+            )
+        outgoing_ref[edge:shards] = (
+            mixed_ref[edge * local_ch :, :].reshape(TAIL, local_ch, block).astype(jnp.bfloat16)
+        )
+        send_back(outgoing_ref, me, back_send_sem, edge, shards)
+
+    @pl.when(jnp.logical_not(is_last))
+    def _():
+        upper_rows(half, shards)
 
     pltpu.make_async_copy(outgoing_ref.at[me], conv_ref.at[me], back_recv_sem).start()
 
@@ -357,7 +410,7 @@
             pltpu.VMEM((half, local_ch, block), jnp.bfloat16),
             pltpu.SemaphoreType.DMA((4,)),
             pltpu.SemaphoreType.DMA,
-            pltpu.SemaphoreType.DMA((4,)),
+            pltpu.SemaphoreType.DMA((shards // TAIL,)),
             pltpu.SemaphoreType.DMA,
             pltpu.SemaphoreType.DMA((2,)),
             pltpu.SemaphoreType.DMA,

time: 29.3 us -> 28.4 us (0.969)
  the two profiles are of different devices: /device:TPU:24 before, /device:TPU:192 now
where the time goes in v5:
time: 28.4 us; the launch traced here: 28.2 us
  Pallas kernels  27.6 us (97%)
  other arithmetic  0.66 us (2%)
    pallas_call x1, Pallas kernels, per_device(): pl.pallas_call(conv_kernel, out_shape=(jax.ShapeDtypeStruct(stacked, jnp....  27.6 us
    convert_element_type x1, other arithmetic, per_device(): return result.astype(jnp.bfloat16)  0.66 us

profile of v5, /device:TPU:192, one launch (start us, length us, event | category | flops | bytes accessed | tf_op | source)
XLA Modules:
  0.0 28.2 jit_solution(14646129580650435374)
XLA Ops:
  0.0 0.0 copy-start
  0.0 27.6 %hyena_conv.1 = (bf16[32,8,128]{2,1,0:T(8,128)(2,1)S(1)}, f32[256,128]{1,0:T(8,128)S(1)}) custom-call(bf16[32,8,128]{2,1,0:T(8,128)(2,1)} %bitcast.5, bf16[32,8,128]{2,1,0:T(8,128)(2,1)} %bitcast.6, f32[8,4096]{1,0:T(8,128)} %filters_hbm.1, f32[256]{0:T(256)} %skip_hbm.1), custom_call_target="tpu_custom_call" | custom-call | tf_op jit(solution)/shard_map/hyena_conv/pallas_call | solution.py:385
  27.6 0.0 copy-done
  27.6 0.7 %fusion.1 = bf16[256,128]{1,0:T(8,128)(2,1)} fusion(f32[256,128]{1,0:T(8,128)S(1)} %get-tuple-element.8, bf16[256,128]{1,0:T(8,128)(2,1)S(1)} %copy-done, bf16[32,8,128]{2,1,0:T(8,128)(2,1)S(1)} %get-tuple-element.7), kind=kLoop, calls=%fused_computation.2 | loop fusion | flops 163840 | bytes 327680 | tf_op jit(solution)/shard_map/convert_element_type | solution.py:431
Async XLA Ops:
  0.0 27.6 %copy-start = (bf16[256,128]{1,0:T(8,128)(2,1)S(1)}, bf16[256,128]{1,0:T(8,128)(2,1)}, u32[]{:S(2)}) copy-start(bf16[256,128]{1,0:T(8,128)(2,1)} %param.5) | copy-start | bytes 196612

commit v6 on v5

--- a/solution.py
+++ b/solution.py
@@ -47,6 +47,7 @@
     low_back_send_sem,
     back_recv_sem,
     last_sem,
+    upper_sem,
 ):
     shards, local_ch, block = gated_ref.shape
     me = lax.axis_index("context")
@@ -62,9 +63,15 @@
     borrows = (upper == 0) & (me + tensor > 0)
     lends = (upper == 1) & (partner + tensor > 0)
 
+    staged = 1 - lax.min(lax.rem(tensor // 2, 4) // 2, 1)
+
     def greet(k, carry):
         peer = lax.rem(me + k, shards)
-        pl.semaphore_signal(barrier, inc=1, device_id=(tensor, peer), device_id_type=MESH)
+
+        @pl.when((upper * staged == 0) | (peer >= half) | (peer + tensor == 0))
+        def _():
+            pl.semaphore_signal(barrier, inc=1, device_id=(tensor, peer), device_id_type=MESH)
+
         return carry
 
     @pl.when(jnp.logical_not(is_last))
@@ -129,7 +136,16 @@
         for c in range(local_ch):
             build_own(c)
 
-    pl.semaphore_wait(barrier, shards - 1 - first_group * lax.min(me, 1))
+    hidden = staged * (1 - upper) * lax.min(me + tensor, 1) * half
+    pl.semaphore_wait(barrier, shards - 1 - first_group * lax.min(me, 1) - hidden)
+
+    @pl.when(upper * staged == 1)
+    def _():
+        def arise(peer, carry):
+            pl.semaphore_signal(upper_sem, inc=1, device_id=(tensor, peer), device_id_type=MESH)
+            return carry
+
+        lax.fori_loop(first_group, half, arise, 0)
 
     @pl.when(is_last)
     def _():
@@ -181,6 +197,10 @@
         @pl.when(borrows)
         def _():
             pltpu.make_async_copy(gated_ref.at[partner], low_arrived_ref.at[me], low_mine).start()
+
+        @pl.when(hidden > 0)
+        def _():
+            pl.semaphore_wait(upper_sem, half)
 
         lax.fori_loop(0, half, send_high, 0)
 
@@ -419,6 +439,7 @@
             pltpu.SemaphoreType.DMA,
             pltpu.SemaphoreType.DMA,
             pltpu.SemaphoreType.REGULAR,
+            pltpu.SemaphoreType.REGULAR,
         ],
         compiler_params=pltpu.CompilerParams(
             collective_id=0, has_side_effects=True, vmem_limit_bytes=40 << 20

time: 28.4 us -> 29.2 us (1.028)
  the two profiles are of different devices: /device:TPU:192 before, /device:TPU:2 now
where the time goes in v6:
time: 29.2 us; the launch traced here: 29.1 us
  Pallas kernels  28.4 us (97%)
  other arithmetic  0.66 us (2%)
    pallas_call x1, Pallas kernels, per_device(): pl.pallas_call(conv_kernel, out_shape=(jax.ShapeDtypeStruct(stacked, jnp....  28.4 us
    convert_element_type x1, other arithmetic, per_device(): return result.astype(jnp.bfloat16)  0.66 us

profile of v6, /device:TPU:2, one launch (start us, length us, event | category | flops | bytes accessed | tf_op | source)
XLA Modules:
  0.0 29.1 jit_solution(7776050218439258226)
XLA Ops:
  0.0 0.0 copy-start
  0.0 28.4 %hyena_conv.1 = (bf16[32,8,128]{2,1,0:T(8,128)(2,1)S(1)}, f32[256,128]{1,0:T(8,128)S(1)}) custom-call(bf16[32,8,128]{2,1,0:T(8,128)(2,1)} %bitcast.5, bf16[32,8,128]{2,1,0:T(8,128)(2,1)} %bitcast.6, f32[8,4096]{1,0:T(8,128)} %filters_hbm.1, f32[256]{0:T(256)} %skip_hbm.1), custom_call_target="tpu_custom_call" | custom-call | tf_op jit(solution)/shard_map/hyena_conv/pallas_call | solution.py:405
  28.4 0.0 copy-done
  28.4 0.7 %fusion.1 = bf16[256,128]{1,0:T(8,128)(2,1)} fusion(f32[256,128]{1,0:T(8,128)S(1)} %get-tuple-element.8, bf16[256,128]{1,0:T(8,128)(2,1)S(1)} %copy-done, bf16[32,8,128]{2,1,0:T(8,128)(2,1)S(1)} %get-tuple-element.7), kind=kLoop, calls=%fused_computation.2 | loop fusion | flops 163840 | bytes 327680 | tf_op jit(solution)/shard_map/convert_element_type | solution.py:452
Async XLA Ops:
  0.0 28.4 %copy-start = (bf16[256,128]{1,0:T(8,128)(2,1)S(1)}, bf16[256,128]{1,0:T(8,128)(2,1)}, u32[]{:S(2)}) copy-start(bf16[256,128]{1,0:T(8,128)(2,1)} %param.5) | copy-start | bytes 196612
